TPU v7x, 32 devices: a whole 2x2x4 slice. The times are simulated.
32 devices in a mesh: view: 4 (over x, core), samp: 8 (over z, y).
Axes of the slice: x: 2, y: 2, z: 4, core: 2. Of those that a mesh axis runs over, the one named last changes fastest.
Arguments:
- view_data: bfloat16 [8, 4096, 2048], P('view', 'samp'), may hold values from -10 to 10
- init_coeffs: float32 [8, 2048, 128], P('view'), may hold values from -0.125 to 0.125
Outputs:
- shared_scores: float32 [4096, 128], P('samp')
- final_coeffs: float32 [8, 2048, 128], P('view', 'samp')
All inputs are finite; a program needn't handle non-finite values.
Results may differ from a plain program's by a relative error of at most 0.005.
Values may be sent and summed in bfloat16 or wider, within the bound.
No kernel may reach another device: no remote copies, remote signals or barrier semaphores. Data moves between devices by JAX's collectives and lax.ppermute only.
A program may use at most 128 MiB of HBM per device.

v0:
```python
import jax
import jax.numpy as jnp
from jax import lax
from jax.sharding import PartitionSpec as P

OUTER = 2
INNER = 2
NS_ITERS = 12
HIGH = lax.Precision.HIGHEST
ridge_weight = 0.1
step_size = 0.5


def newton_inverse(gram):
    size_k = gram.shape[0]
    eye_mat = jnp.eye(size_k, dtype=jnp.float32)
    shrunk = gram + jnp.trace(gram) / size_k * eye_mat
    scale = jnp.sqrt(jnp.sum(shrunk * shrunk))
    approx = shrunk / scale
    inverse = eye_mat
    for turn in range(NS_ITERS):
        factor = 0.5 * (3.0 * eye_mat - jnp.dot(inverse, approx, precision=HIGH))
        approx = jnp.dot(approx, factor, precision=HIGH)
        inverse = jnp.dot(factor, inverse, precision=HIGH)
    return (inverse, scale)


def make_scores(view_data, coeffs_low, total):
    local_sum = jnp.zeros((view_data.shape[1], coeffs_low.shape[2]), jnp.float32)
    for member in range(view_data.shape[0]):
        local_sum = local_sum + jnp.dot(
            view_data[member], coeffs_low[member], preferred_element_type=jnp.float32
        )
    summed = lax.psum(local_sum, "view")
    gram = lax.psum(jnp.dot(summed.T, summed, precision=HIGH), "samp")
    inverse, scale = newton_inverse(gram)
    return jnp.dot(summed, inverse, precision=HIGH) * jnp.sqrt(total / scale)


def grad_term(samples, weights_low, scores):
    resid = (jnp.dot(samples, weights_low, preferred_element_type=jnp.float32) - scores).astype(
        jnp.bfloat16
    )
    return lax.dot_general(
        samples, resid, (((0,), (0,)), ((), ())), preferred_element_type=jnp.float32
    )


def body(view_data, init_coeffs):
    total = view_data.shape[1] * lax.axis_size("samp")
    row_count = init_coeffs.shape[1] // lax.axis_size("samp")
    row_start = lax.axis_index("samp") * row_count
    own_coeffs = lax.dynamic_slice_in_dim(init_coeffs, row_start, row_count, 1)
    coeffs_low = init_coeffs.astype(jnp.bfloat16)
    scores = make_scores(view_data, coeffs_low, total)
    for outer_step in range(OUTER):
        for inner_step in range(INNER):
            terms = jnp.stack(
                [
                    grad_term(view_data[member], coeffs_low[member], scores)
                    for member in range(view_data.shape[0])
                ]
            )
            summed_grad = lax.psum_scatter(terms, "samp", scatter_dimension=1, tiled=True)
            own_coeffs = own_coeffs - step_size * (summed_grad / total + ridge_weight * own_coeffs)
            coeffs_low = lax.all_gather(own_coeffs.astype(jnp.bfloat16), "samp", axis=1, tiled=True)
        scores = make_scores(view_data, coeffs_low, total)
    return (scores, own_coeffs)


def solution(mesh):
    in_specs = (P("view", "samp", None), P("view", None, None))
    out_specs = (P("samp", None), P("view", "samp", None))
    return jax.shard_map(body, mesh=mesh, in_specs=in_specs, out_specs=out_specs, check_vma=False)
```

profile of v0, /device:TPU:0, one launch (start us, length us, event | category | flops | bytes accessed | tf_op | source)
XLA Modules:
  0.0 856.1 jit_solution(11644975215844309981)
XLA Ops:
  7.2 1.9 convert_element_type.42
  9.1 2.3 fusion.12
  11.4 1.4 fusion.163
  12.9 35.1 %all-reduce.7.cloned.1.call-done = f32[512,128]{1,0:T(8,128)} async-done(((f32[512,128]{1,0:T(8,128)}), f32[512,128]{1,0:T(8,128)}) %all-reduce.7.cloned.1.call-update) | async-done | bytes 262160 | tf_op jit(solution)/shard_map/psum | solution.py:34
  48.0 2.2 fusion.165
  50.4 70.9 %all-reduce.9.cloned.1.call-done = f32[128,128]{1,0:T(8,128)} async-done(((f32[128,128]{1,0:T(8,128)}), f32[128,128]{1,0:T(8,128)}) %all-reduce.9.cloned.1.call-update) | async-done | bytes 65552 | tf_op jit(solution)/shard_map/psum | solution.py:35
  121.3 1.5 select_reduce_fusion.2
  123.4 1.5 multiply_reduce_fusion.2
  125.6 1.0 fusion.119
  126.8 1.1 fusion.152
  127.9 0.2 fusion.118
  129.8 0.2 fusion.115
  134.8 0.4 convolution_multiply_fusion.2
  135.1 2.3 convolution_bitcast_fusion.6
  137.6 0.5 convolution_bitcast_fusion.7
  138.0 1.5 pad_maximum_fusion
  139.6 1.0 constant_dynamic-slice_fusion
  140.7 67.8 %reduce-scatter.5.cloned.1.call-done = f32[2,256,128]{1,2,0:T(8,128)} async-done(((f32[2,2048,128]{1,2,0:T(8,128)}), f32[2,256,128]{1,2,0:T(8,128)}) %reduce-scatter.5.cloned.1.call-update) | async-done | bytes 262160 | tf_op jit(solution)/shard_map/reduce_scatter | solution.py:64
  208.5 1.7 fusion.144
  210.3 39.2 %all-gather.5.cloned.1.call-done = bf16[2,2048,128]{1,2,0:T(8,128)(2,1)} async-done(((bf16[2,256,128]{1,2,0:T(8,128)(2,1)}), bf16[2,2048,128]{1,2,0:T(8,128)(2,1)}) %all-gather.5.cloned.1.call-update) | async-done | bytes 1048592 | tf_op jit(solution)/shard_map/all_gather | solution.py:66
  249.5 4.0 convolution_bitcast_fusion.4
  253.4 4.0 convolution_bitcast_fusion.5
  257.4 1.5 pad_maximum_fusion.1
  259.0 68.0 %reduce-scatter.7.cloned.1.call-done = f32[2,256,128]{1,2,0:T(8,128)} async-done(((f32[2,2048,128]{1,2,0:T(8,128)}), f32[2,256,128]{1,2,0:T(8,128)}) %reduce-scatter.7.cloned.1.call-update) | async-done | bytes 262160 | tf_op jit(solution)/shard_map/reduce_scatter | solution.py:64
  327.0 1.7 fusion.162
  328.7 39.1 %all-gather.7.cloned.1.call-done = bf16[2,2048,128]{1,2,0:T(8,128)(2,1)} async-done(((bf16[2,256,128]{1,2,0:T(8,128)(2,1)}), bf16[2,2048,128]{1,2,0:T(8,128)(2,1)}) %all-gather.7.cloned.1.call-update) | async-done | bytes 1048592 | tf_op jit(solution)/shard_map/all_gather | solution.py:66
  367.9 2.7 fusion.55
  370.6 3.1 fusion.164
  373.7 0.2 all-reduce.13.cloned.1.call-start
  374.0 31.2 %all-reduce.11.cloned.1.call-done = f32[512,128]{0,1:T(8,128)} async-done(((f32[512,128]{0,1:T(8,128)}), f32[512,128]{0,1:T(8,128)}) %all-reduce.11.cloned.1.call-update) | async-done | bytes 262160 | tf_op jit(solution)/shard_map/psum | solution.py:34
  405.2 2.0 fusion.187
  407.3 71.1 %all-reduce.13.cloned.1.call-done = f32[128,128]{1,0:T(8,128)} async-done(((f32[128,128]{1,0:T(8,128)}), f32[128,128]{1,0:T(8,128)}) %all-reduce.13.cloned.1.call-update) | async-done | bytes 65552 | tf_op jit(solution)/shard_map/psum | solution.py:35
  478.4 1.5 select_reduce_fusion.1
  480.6 1.5 multiply_reduce_fusion.1
  482.8 1.0 fusion.107
  484.0 1.1 fusion.149
  485.0 0.2 fusion.106
  487.6 0.2 fusion.102
  490.8 0.2 fusion.97
  491.9 0.4 convolution_multiply_fusion.1
  492.3 2.3 convolution_bitcast_fusion.2
  494.7 0.4 convolution_bitcast_fusion.3
  495.2 1.5 pad_maximum_fusion.2
  496.7 69.1 %reduce-scatter.9.cloned.1.call-done = f32[2,256,128]{1,2,0:T(8,128)} async-done(((f32[2,2048,128]{1,2,0:T(8,128)}), f32[2,256,128]{1,2,0:T(8,128)}) %reduce-scatter.9.cloned.1.call-update) | async-done | bytes 262160 | tf_op jit(solution)/shard_map/reduce_scatter | solution.py:64
  565.8 1.7 fusion.145
  567.5 39.2 %all-gather.9.cloned.1.call-done = bf16[2,2048,128]{1,2,0:T(8,128)(2,1)} async-done(((bf16[2,256,128]{1,2,0:T(8,128)(2,1)}), bf16[2,2048,128]{1,2,0:T(8,128)(2,1)}) %all-gather.9.cloned.1.call-update) | async-done | bytes 1048592 | tf_op jit(solution)/shard_map/all_gather | solution.py:66
  606.7 3.6 convolution_bitcast_fusion
  610.3 3.6 convolution_bitcast_fusion.1
  613.9 1.5 pad_maximum_fusion.3
  615.5 68.0 %reduce-scatter.11.cloned.1.call-done = f32[2,256,128]{1,2,0:T(8,128)} async-done(((f32[2,2048,128]{1,2,0:T(8,128)}), f32[2,256,128]{1,2,0:T(8,128)}) %reduce-scatter.11.cloned.1.call-update) | async-done | bytes 262160 | tf_op jit(solution)/shard_map/reduce_scatter | solution.py:64
  683.5 1.7 fusion.161
  685.3 39.1 %all-gather.11.cloned.1.call-done = bf16[2,2048,128]{1,2,0:T(8,128)(2,1)} async-done(((bf16[2,256,128]{1,2,0:T(8,128)(2,1)}), bf16[2,2048,128]{1,2,0:T(8,128)(2,1)}) %all-gather.11.cloned.1.call-update) | async-done | bytes 1048592 | tf_op jit(solution)/shard_map/all_gather | solution.py:66
  724.4 2.7 fusion
  727.1 3.1 fusion.46
  730.3 0.3 all-reduce.17.cloned.1.call-start
  730.5 31.2 %all-reduce.15.cloned.1.call-done = f32[512,128]{0,1:T(8,128)} async-done(((f32[512,128]{0,1:T(8,128)}), f32[512,128]{0,1:T(8,128)}) %all-reduce.15.cloned.1.call-update) | async-done | bytes 262160 | tf_op jit(solution)/shard_map/psum | solution.py:34
  761.7 2.0 fusion.209
  763.8 0.8 copy.6
  764.6 70.2 %all-reduce.17.cloned.1.call-done = f32[128,128]{1,0:T(8,128)} async-done(((f32[128,128]{1,0:T(8,128)}), f32[128,128]{1,0:T(8,128)}) %all-reduce.17.cloned.1.call-update) | async-done | bytes 65552 | tf_op jit(solution)/shard_map/psum | solution.py:35
  834.8 1.5 select_reduce_fusion
  837.0 1.5 multiply_reduce_fusion
  839.2 1.0 fusion.95
  840.4 1.1 fusion.146
  848.3 1.3 convolution_multiply_fusion
  (141 shorter events, 20.3 us)
Async XLA Ops:
  7.2 40.9 %all-reduce.7.cloned.1.call-start = ((), (), s32[]{:S(2)}) async-start(), calls=%async_computation.4 | async-start | bytes 524288 | tf_op jit(solution)/shard_map/psum | solution.py:34
  7.2 4.2 copy-start
  12.9 108.4 %all-reduce.9.cloned.1.call-start = ((), (), s32[]{:S(2)}) async-start(), calls=%async_computation.5 | async-start | bytes 131072 | tf_op jit(solution)/shard_map/psum | solution.py:35
  50.3 158.2 %reduce-scatter.5.cloned.1.call-start = ((), (), s32[]{:S(2)}) async-start(), calls=%async_computation.6 | async-start | bytes 2359296 | tf_op jit(solution)/shard_map/reduce_scatter | solution.py:64
  130.2 4.5 copy-start.4
  134.7 2.8 copy-start.1
  139.6 109.9 %all-gather.5.cloned.1.call-start = ((), (), s32[]{:S(2)}) async-start(), calls=%async_computation.7 | async-start | bytes 1179648 | tf_op jit(solution)/shard_map/all_gather | solution.py:66
  210.2 116.8 %reduce-scatter.7.cloned.1.call-start = ((), (), s32[]{:S(2)}) async-start(), calls=%async_computation.8 | async-start | bytes 2359296 | tf_op jit(solution)/shard_map/reduce_scatter | solution.py:64
  258.9 68.1 %copy-start.6 = (f32[2,256,128]{1,2,0:T(8,128)S(1)}, f32[2,256,128]{1,2,0:T(8,128)}, u32[]{:S(2)}) copy-start(f32[2,256,128]{1,2,0:T(8,128)} %reduce-scatter.5.cloned.1.call-done) | copy-start | bytes 786436
  258.9 109.0 %all-gather.7.cloned.1.call-start = ((), (), s32[]{:S(2)}) async-start(), calls=%async_computation.9 | async-start | bytes 1179648 | tf_op jit(solution)/shard_map/all_gather | solution.py:66
  328.7 76.5 %all-reduce.11.cloned.1.call-start = ((), (), s32[]{:S(2)}) async-start(), calls=%async_computation.10 | async-start | bytes 524288 | tf_op jit(solution)/shard_map/psum | solution.py:34
  367.9 2.7 copy-start.8
  373.7 104.7 %all-reduce.13.cloned.1.call-start = ((), (), s32[]{:S(2)}) async-start(), calls=%async_computation.11 | async-start | bytes 131072 | tf_op jit(solution)/shard_map/psum | solution.py:35
  407.3 158.5 %reduce-scatter.9.cloned.1.call-start = ((), (), s32[]{:S(2)}) async-start(), calls=%async_computation.12 | async-start | bytes 2359296 | tf_op jit(solution)/shard_map/reduce_scatter | solution.py:64
  487.4 4.5 copy-start.5
  491.9 2.8 copy-start.2
  496.7 110.0 %all-gather.9.cloned.1.call-start = ((), (), s32[]{:S(2)}) async-start(), calls=%async_computation.13 | async-start | bytes 1179648 | tf_op jit(solution)/shard_map/all_gather | solution.py:66
  567.5 116.0 %reduce-scatter.11.cloned.1.call-start = ((), (), s32[]{:S(2)}) async-start(), calls=%async_computation.14 | async-start | bytes 2359296 | tf_op jit(solution)/shard_map/reduce_scatter | solution.py:64
  615.4 68.1 %copy-start.7 = (f32[2,256,128]{1,2,0:T(8,128)S(1)}, f32[2,256,128]{1,2,0:T(8,128)}, u32[]{:S(2)}) copy-start(f32[2,256,128]{1,2,0:T(8,128)} %reduce-scatter.9.cloned.1.call-done) | copy-start | bytes 786436
  615.4 109.0 %all-gather.11.cloned.1.call-start = ((), (), s32[]{:S(2)}) async-start(), calls=%async_computation.15 | async-start | bytes 1179648 | tf_op jit(solution)/shard_map/all_gather | solution.py:66
  685.2 76.5 %all-reduce.15.cloned.1.call-start = ((), (), s32[]{:S(2)}) async-start(), calls=%async_computation.16 | async-start | bytes 524288 | tf_op jit(solution)/shard_map/psum | solution.py:34
  724.4 2.7 copy-start.9
  730.3 104.6 %all-reduce.17.cloned.1.call-start = ((), (), s32[]{:S(2)}) async-start(), calls=%async_computation.17 | async-start | bytes 131072 | tf_op jit(solution)/shard_map/psum | solution.py:35
  843.8 4.5 copy-start.3
Sparse Core Ops, SparseCore 0:
  13.0 35.0 all-reduce.6
  52.0 69.2 all-reduce.8
  139.7 68.8 reduce-scatter.4
  211.0 38.3 all-gather.4
  259.0 67.8 reduce-scatter.6
  329.4 38.4 all-gather.6
  373.9 31.2 all-reduce.10
  409.2 69.2 all-reduce.12
  496.8 68.9 reduce-scatter.8
  568.2 38.3 all-gather.8
  615.6 67.9 reduce-scatter.10
  686.0 38.3 all-gather.10
  730.4 31.2 all-reduce.14
  765.6 69.2 all-reduce.16
where the time goes:
time: 857 us; the launch traced here: 856 us
  waiting for transfers between devices  740 us (86%)
  matrix products  70.7 us (8%)
  other arithmetic  23.3 us (3%)
  between operations  19.3 us (2%)
    reduce_scatter x4, waiting for transfers between devices, body(): lax.psum_scatter(terms, 'samp', scatter_dimension=1, tiled=True)  273 us
    psum x3, waiting for transfers between devices, make_scores(): gram = lax.psum(jnp.dot(summed.T, summed, precision=HIGH), 'samp')  212 us
    all_gather x4, waiting for transfers between devices, body(): lax.all_gather(own_coeffs.astype(jnp.bfloat16), 'samp', axis=1, tiled=True)  157 us
    psum x3, waiting for transfers between devices, make_scores(): summed = lax.psum(local_sum, 'view')  97.5 us
    dot_general x8, matrix products, grad_term(): lax.dot_general(samples, resid, (((0,), (0,)), ((), ())), preferred_eleme...  20.6 us
  transfers between devices with their start and end apart: 14, of which 14 were waited for; matrix products, arithmetic and copies ran while one was open for 0% of the time, Pallas kernels for 0%

commit v1 on v0

--- a/solution.py
+++ b/solution.py
@@ -31,7 +31,7 @@
         local_sum = local_sum + jnp.dot(
             view_data[member], coeffs_low[member], preferred_element_type=jnp.float32
         )
-    summed = lax.psum(local_sum, "view")
+    summed = jnp.sum(lax.all_gather(local_sum, "view"), axis=0)
     gram = lax.psum(jnp.dot(summed.T, summed, precision=HIGH), "samp")
     inverse, scale = newton_inverse(gram)
     return jnp.dot(summed, inverse, precision=HIGH) * jnp.sqrt(total / scale)

time: 857 us -> 811 us (0.946)
  waiting for transfers between devices: 740 us -> 690 us
    psum x3 -> x0, waiting for transfers between devices: 97.5 us -> none  [make_scores(): summed = lax.psum(local_sum, 'view')]
    all_gather x0 -> x3, waiting for transfers between devices: none -> 50.8 us  [make_scores(): summed = jnp.sum(lax.all_gather(local_sum, 'view'), axis=0)]
where the time goes in v1:
time: 811 us; the launch traced here: 810 us
  waiting for transfers between devices  690 us (85%)
  matrix products  67.5 us (8%)
  other arithmetic  25.9 us (3%)
  between operations  19.2 us (2%)
    reduce_scatter x4, waiting for transfers between devices, body(): lax.psum_scatter(terms, 'samp', scatter_dimension=1, tiled=True)  273 us
    psum x3, waiting for transfers between devices, make_scores(): gram = lax.psum(jnp.dot(summed.T, summed, precision=HIGH), 'samp')  209 us
    all_gather x4, waiting for transfers between devices, body(): lax.all_gather(own_coeffs.astype(jnp.bfloat16), 'samp', axis=1, tiled=True)  157 us
    all_gather x3, waiting for transfers between devices, make_scores(): summed = jnp.sum(lax.all_gather(local_sum, 'view'), axis=0)  50.8 us
    dot_general x8, matrix products, grad_term(): lax.dot_general(samples, resid, (((0,), (0,)), ((), ())), preferred_eleme...  20.6 us
  transfers between devices with their start and end apart: 14, of which 14 were waited for; matrix products, arithmetic and copies ran while one was open for 0% of the time, Pallas kernels for 0%

profile of v1, /device:TPU:0, one launch (start us, length us, event | category | flops | bytes accessed | tf_op | source)
XLA Modules:
  0.0 809.9 jit_solution(13586449834848094274)
XLA Ops:
  7.2 1.9 convert_element_type.42
  9.1 2.3 fusion.12
  11.4 1.4 fusion.163
  12.9 19.5 %all-gather.19.cloned.1.call-done = f32[2048,128]{1,0:T(8,128)} async-done(((f32[512,128]{1,0:T(8,128)}), f32[2048,128]{1,0:T(8,128)}) %all-gather.19.cloned.1.call-update) | async-done | bytes 1048592 | tf_op jit(solution)/shard_map/all_gather | solution.py:34
  32.4 1.3 reduce_sum.76
  33.8 1.2 fusion.165
  35.1 70.7 %all-reduce.4.cloned.1.call-done = f32[128,128]{1,0:T(8,128)} async-done(((f32[128,128]{1,0:T(8,128)}), f32[128,128]{1,0:T(8,128)}) %all-reduce.4.cloned.1.call-update) | async-done | bytes 65552 | tf_op jit(solution)/shard_map/psum | solution.py:35
  105.7 1.5 select_reduce_fusion.2
  107.8 1.5 multiply_reduce_fusion.2
  110.0 1.0 fusion.119
  111.2 1.1 fusion.152
  119.2 0.4 convolution_multiply_fusion.2
  119.5 2.3 convolution_bitcast_fusion.6
  122.0 0.5 convolution_bitcast_fusion.7
  122.4 1.5 pad_maximum_fusion
  124.0 1.0 constant_dynamic-slice_fusion
  125.1 68.1 %reduce-scatter.5.cloned.1.call-done = f32[2,256,128]{1,2,0:T(8,128)} async-done(((f32[2,2048,128]{1,2,0:T(8,128)}), f32[2,256,128]{1,2,0:T(8,128)}) %reduce-scatter.5.cloned.1.call-update) | async-done | bytes 262160 | tf_op jit(solution)/shard_map/reduce_scatter | solution.py:64
  193.3 1.7 fusion.144
  195.0 39.2 %all-gather.11.cloned.1.call-done = bf16[2,2048,128]{1,2,0:T(8,128)(2,1)} async-done(((bf16[2,256,128]{1,2,0:T(8,128)(2,1)}), bf16[2,2048,128]{1,2,0:T(8,128)(2,1)}) %all-gather.11.cloned.1.call-update) | async-done | bytes 1048592 | tf_op jit(solution)/shard_map/all_gather | solution.py:66
  234.2 4.0 convolution_bitcast_fusion.4
  238.1 4.0 convolution_bitcast_fusion.5
  242.1 1.5 pad_maximum_fusion.1
  243.7 68.0 %reduce-scatter.7.cloned.1.call-done = f32[2,256,128]{1,2,0:T(8,128)} async-done(((f32[2,2048,128]{1,2,0:T(8,128)}), f32[2,256,128]{1,2,0:T(8,128)}) %reduce-scatter.7.cloned.1.call-update) | async-done | bytes 262160 | tf_op jit(solution)/shard_map/reduce_scatter | solution.py:64
  311.7 1.7 fusion.162
  313.4 39.1 %all-gather.13.cloned.1.call-done = bf16[2,2048,128]{1,2,0:T(8,128)(2,1)} async-done(((bf16[2,256,128]{1,2,0:T(8,128)(2,1)}), bf16[2,2048,128]{1,2,0:T(8,128)(2,1)}) %all-gather.13.cloned.1.call-update) | async-done | bytes 1048592 | tf_op jit(solution)/shard_map/all_gather | solution.py:66
  352.6 2.7 fusion.55
  355.3 3.1 fusion.164
  358.4 0.2 all-reduce.6.cloned.1.call-start
  358.7 15.6 %all-gather.21.cloned.1.call-done = f32[2048,128]{0,1:T(8,128)} async-done(((f32[512,128]{0,1:T(8,128)}), f32[2048,128]{0,1:T(8,128)}) %all-gather.21.cloned.1.call-update) | async-done | bytes 1048592 | tf_op jit(solution)/shard_map/all_gather | solution.py:34
  374.3 1.9 reshape.5
  376.2 0.6 reduce_sum.79
  376.9 1.0 fusion.187
  377.9 69.6 %all-reduce.6.cloned.1.call-done = f32[128,128]{1,0:T(8,128)} async-done(((f32[128,128]{1,0:T(8,128)}), f32[128,128]{1,0:T(8,128)}) %all-reduce.6.cloned.1.call-update) | async-done | bytes 65552 | tf_op jit(solution)/shard_map/psum | solution.py:35
  447.6 1.5 select_reduce_fusion.1
  449.7 1.5 multiply_reduce_fusion.1
  451.9 1.0 fusion.107
  453.1 1.1 fusion.149
  461.0 0.4 convolution_multiply_fusion.1
  461.4 2.2 convolution_bitcast_fusion.2
  463.8 0.4 convolution_bitcast_fusion.3
  464.3 1.5 pad_maximum_fusion.2
  465.8 68.9 %reduce-scatter.9.cloned.1.call-done = f32[2,256,128]{1,2,0:T(8,128)} async-done(((f32[2,2048,128]{1,2,0:T(8,128)}), f32[2,256,128]{1,2,0:T(8,128)}) %reduce-scatter.9.cloned.1.call-update) | async-done | bytes 262160 | tf_op jit(solution)/shard_map/reduce_scatter | solution.py:64
  534.8 1.7 fusion.145
  536.5 39.2 %all-gather.15.cloned.1.call-done = bf16[2,2048,128]{1,2,0:T(8,128)(2,1)} async-done(((bf16[2,256,128]{1,2,0:T(8,128)(2,1)}), bf16[2,2048,128]{1,2,0:T(8,128)(2,1)}) %all-gather.15.cloned.1.call-update) | async-done | bytes 1048592 | tf_op jit(solution)/shard_map/all_gather | solution.py:66
  575.7 3.6 convolution_bitcast_fusion
  579.3 3.6 convolution_bitcast_fusion.1
  582.9 1.5 pad_maximum_fusion.3
  584.5 68.4 %reduce-scatter.11.cloned.1.call-done = f32[2,256,128]{1,2,0:T(8,128)} async-done(((f32[2,2048,128]{1,2,0:T(8,128)}), f32[2,256,128]{1,2,0:T(8,128)}) %reduce-scatter.11.cloned.1.call-update) | async-done | bytes 262160 | tf_op jit(solution)/shard_map/reduce_scatter | solution.py:64
  652.9 1.7 fusion.161
  654.6 39.1 %all-gather.17.cloned.1.call-done = bf16[2,2048,128]{1,2,0:T(8,128)(2,1)} async-done(((bf16[2,256,128]{1,2,0:T(8,128)(2,1)}), bf16[2,2048,128]{1,2,0:T(8,128)(2,1)}) %all-gather.17.cloned.1.call-update) | async-done | bytes 1048592 | tf_op jit(solution)/shard_map/all_gather | solution.py:66
  693.8 2.7 fusion
  696.5 3.1 fusion.46
  699.6 0.3 all-reduce.8.cloned.1.call-start
  699.9 15.6 %all-gather.23.cloned.1.call-done = f32[2048,128]{0,1:T(8,128)} async-done(((f32[512,128]{0,1:T(8,128)}), f32[2048,128]{0,1:T(8,128)}) %all-gather.23.cloned.1.call-update) | async-done | bytes 1048592 | tf_op jit(solution)/shard_map/all_gather | solution.py:34
  715.5 1.9 reshape.6
  717.4 0.6 reduce_sum.82
  718.0 1.0 fusion.209
  719.1 0.8 copy.9
  719.9 68.7 %all-reduce.8.cloned.1.call-done = f32[128,128]{1,0:T(8,128)} async-done(((f32[128,128]{1,0:T(8,128)}), f32[128,128]{1,0:T(8,128)}) %all-reduce.8.cloned.1.call-update) | async-done | bytes 65552 | tf_op jit(solution)/shard_map/psum | solution.py:35
  788.6 1.5 select_reduce_fusion
  790.7 1.5 multiply_reduce_fusion
  792.9 1.0 fusion.95
  794.2 1.1 fusion.146
  802.0 1.3 convolution_multiply_fusion
  (140 shorter events, 21.3 us)
Async XLA Ops:
  7.2 25.3 %all-gather.19.cloned.1.call-start = ((), (), s32[]{:S(2)}) async-start(), calls=%async_computation.15 | async-start | bytes 1310720 | tf_op jit(solution)/shard_map/all_gather | solution.py:34
  7.2 4.2 copy-start
  12.9 92.9 %all-reduce.4.cloned.1.call-start = ((), (), s32[]{:S(2)}) async-start(), calls=%async_computation.4 | async-start | bytes 131072 | tf_op jit(solution)/shard_map/psum | solution.py:35
  35.0 158.3 %reduce-scatter.5.cloned.1.call-start = ((), (), s32[]{:S(2)}) async-start(), calls=%async_computation.5 | async-start | bytes 2359296 | tf_op jit(solution)/shard_map/reduce_scatter | solution.py:64
  119.1 2.8 copy-start.1
  124.0 110.2 %all-gather.11.cloned.1.call-start = ((), (), s32[]{:S(2)}) async-start(), calls=%async_computation.6 | async-start | bytes 1179648 | tf_op jit(solution)/shard_map/all_gather | solution.py:66
  194.9 116.7 %reduce-scatter.7.cloned.1.call-start = ((), (), s32[]{:S(2)}) async-start(), calls=%async_computation.7 | async-start | bytes 2359296 | tf_op jit(solution)/shard_map/reduce_scatter | solution.py:64
  243.6 68.1 %copy-start.3 = (f32[2,256,128]{1,2,0:T(8,128)S(1)}, f32[2,256,128]{1,2,0:T(8,128)}, u32[]{:S(2)}) copy-start(f32[2,256,128]{1,2,0:T(8,128)} %reduce-scatter.5.cloned.1.call-done) | copy-start | bytes 786436
  243.6 109.0 %all-gather.13.cloned.1.call-start = ((), (), s32[]{:S(2)}) async-start(), calls=%async_computation.8 | async-start | bytes 1179648 | tf_op jit(solution)/shard_map/all_gather | solution.py:66
  313.4 60.9 %all-gather.21.cloned.1.call-start = ((), (), s32[]{:S(2)}) async-start(), calls=%async_computation.16 | async-start | bytes 1310720 | tf_op jit(solution)/shard_map/all_gather | solution.py:34
  352.6 2.7 copy-start.5
  358.4 89.1 %all-reduce.6.cloned.1.call-start = ((), (), s32[]{:S(2)}) async-start(), calls=%async_computation.9 | async-start | bytes 131072 | tf_op jit(solution)/shard_map/psum | solution.py:35
  377.9 156.9 %reduce-scatter.9.cloned.1.call-start = ((), (), s32[]{:S(2)}) async-start(), calls=%async_computation.10 | async-start | bytes 2359296 | tf_op jit(solution)/shard_map/reduce_scatter | solution.py:64
  461.0 2.8 copy-start.2
  465.8 109.9 %all-gather.15.cloned.1.call-start = ((), (), s32[]{:S(2)}) async-start(), calls=%async_computation.11 | async-start | bytes 1179648 | tf_op jit(solution)/shard_map/all_gather | solution.py:66
  536.4 116.4 %reduce-scatter.11.cloned.1.call-start = ((), (), s32[]{:S(2)}) async-start(), calls=%async_computation.12 | async-start | bytes 2359296 | tf_op jit(solution)/shard_map/reduce_scatter | solution.py:64
  584.4 68.4 %copy-start.4 = (f32[2,256,128]{1,2,0:T(8,128)S(1)}, f32[2,256,128]{1,2,0:T(8,128)}, u32[]{:S(2)}) copy-start(f32[2,256,128]{1,2,0:T(8,128)} %reduce-scatter.9.cloned.1.call-done) | copy-start | bytes 786436
  584.4 109.3 %all-gather.17.cloned.1.call-start = ((), (), s32[]{:S(2)}) async-start(), calls=%async_computation.13 | async-start | bytes 1179648 | tf_op jit(solution)/shard_map/all_gather | solution.py:66
  654.6 60.9 %all-gather.23.cloned.1.call-start = ((), (), s32[]{:S(2)}) async-start(), calls=%async_computation.17 | async-start | bytes 1310720 | tf_op jit(solution)/shard_map/all_gather | solution.py:34
  693.8 2.7 copy-start.6
  699.6 89.0 %all-reduce.8.cloned.1.call-start = ((), (), s32[]{:S(2)}) async-start(), calls=%async_computation.14 | async-start | bytes 131072 | tf_op jit(solution)/shard_map/psum | solution.py:35
Sparse Core Ops, SparseCore 0:
  13.0 19.4 all-gather.18
  36.4 69.2 all-reduce.3
  124.1 69.1 reduce-scatter.4
  195.7 38.3 all-gather.10
  243.7 67.8 reduce-scatter.6
  314.1 38.4 all-gather.12
  358.6 15.6 all-gather.20
  378.3 69.2 all-reduce.5
  465.9 68.8 reduce-scatter.8
  537.2 38.4 all-gather.14
  584.6 68.2 reduce-scatter.10
  655.3 38.4 all-gather.16
  699.7 15.6 all-gather.22
  719.3 69.2 all-reduce.7
